TPU v7x, 32 devices: a whole 2x2x4 slice. The times are simulated.
32 devices in a mesh: ctx: 2 (over y), state: 4 (over z), expert: 4 (over x, core).
Axes of the slice: x: 2, y: 2, z: 4, core: 2. Of those that a mesh axis runs over, the one named last changes fastest.
Arguments:
- tokens: bfloat16 [256, 8192], P('ctx', ('state', 'expert')), may hold values from -6 to 6
- ssm_input: bfloat16 [256, 16384], P('ctx', ('state', 'expert')), may hold values from -6 to 6
- in_b: bfloat16 [256, 128], P('ctx'), may hold values from -1.75 to 1.75
- in_c: bfloat16 [256, 128], P('ctx'), may hold values from -1.75 to 1.75
- decay_log: float32 [256, 64], P('ctx', ('state', 'expert')), may hold values from -0.6 to 0, as said below
- skip_gain: float32 [64], P(('state', 'expert')), may hold values from 0.1 to 1.9
- out_proj: bfloat16 [16384, 8192], P(('state', 'expert'), 'ctx'), may hold values from -0.046875 to 0.046875
- norm_gain: float32 [8192], P(('state', 'expert')), may hold values from 0.1 to 1.9
- routes: int32 [256, 2], P('ctx'), may hold values from 0 to 3, all different within a row; in each aligned block of 128 rows (0 to 127, 128 to 255, ...) at most 80 rows name the same one
- route_gate: float32 [256, 2], P('ctx'), may hold values from 0.2 to 1
- w_gate: bfloat16 [4, 8192, 12288], P('expert', None, ('ctx', 'state')), may hold values from -0.0625 to 0.0625
- w_up: bfloat16 [4, 8192, 12288], P('expert', None, ('ctx', 'state')), may hold values from -0.0625 to 0.0625
- w_down: bfloat16 [4, 12288, 8192], P('expert', ('ctx', 'state')), may hold values from -0.0546875 to 0.0546875
Outputs:
- block_out: bfloat16 [256, 8192], P('ctx', ('state', 'expert'))
Inputs may be any that keep to these rules, and one draw needn't show every extreme that they name: decay_log is never positive. `routes`: in each block of 128 rows (the rows of one index of ctx) no expert is named by more than 80 rows, and in some block one expert is named by exactly 80 rows.
All inputs are finite; a program needn't handle non-finite values.
Results may differ from a plain program's by a relative error of at most 0.017.
Values may be sent and summed in bfloat16 or wider, within the bound.
A program may use at most 192 MiB of HBM per device.

v0:
```python
import jax
import jax.numpy as jnp
from jax import lax
from jax.sharding import PartitionSpec as P

D = 8192
MOST = 80


norm_epsilon = 1e-05


def carried_in(array, axis, join, neutral):
    place = lax.axis_index(axis)
    gathered = jax.tree.map(
        lambda a, kind: lax.all_gather(a.astype(kind), axis), array, (jnp.bfloat16, jnp.bfloat16)
    )
    state = jax.tree.map(lambda a, e: jnp.zeros_like(a) + jnp.asarray(e, a.dtype), array, neutral)

    def one(lap, state):
        return join(
            state,
            jax.tree.map(
                lambda a, own: lax.dynamic_index_in_dim(a, lap, 0, False).astype(own.dtype),
                gathered,
                array,
            ),
        )

    return lax.fori_loop(0, place, one, state)


def block_terms(ssm_input, in_b, in_c, decay_log):
    length = decay_log.shape[0]
    heads_here = decay_log.shape[1]
    width = ssm_input.shape[1] // heads_here
    values = ssm_input.astype(jnp.float32).reshape(length, heads_here, width)
    cumulative = jnp.cumsum(decay_log, axis=0)
    inflow = jnp.sqrt(-jnp.expm1(2.0 * decay_log))
    intersection = jnp.dot(in_c, in_b.T, preferred_element_type=jnp.float32)
    causal = jnp.arange(length)[:, None] >= jnp.arange(length)[None, :]
    spread = cumulative[:, None, :] - cumulative[None, :, :]
    fading = jnp.where(causal[:, :, None], jnp.exp(jnp.minimum(spread, 0.0)), 0.0)
    mixing = intersection[:, :, None] * fading * inflow[None, :, :]
    within = jnp.einsum("tsh,shp->thp", mixing, values, precision=lax.Precision.HIGHEST)
    tail = jnp.exp(cumulative[-1][None, :] - cumulative) * inflow
    state_here = jnp.einsum(
        "sn,sh,shp->hnp", in_b.astype(jnp.float32), tail, values, precision=lax.Precision.HIGHEST
    )
    return (within, state_here, cumulative, values)


def finish_heads(within, carried, cumulative, values, in_c, skip_gain):
    outer = jnp.einsum(
        "tn,hnp->thp", in_c.astype(jnp.float32), carried, precision=lax.Precision.HIGHEST
    )
    result = within + jnp.exp(cumulative)[:, :, None] * outer + skip_gain[None, :, None] * values
    return result.reshape(result.shape[0], -1).astype(jnp.bfloat16)


def route_tables(routes, route_gate, experts, most):
    onehot = (routes[:, :, None] == jnp.arange(experts, dtype=jnp.int32)[None, None, :]).astype(
        jnp.int32
    )
    flat = onehot.reshape(-1, experts)
    before = jnp.cumsum(flat, axis=0, dtype=jnp.int32) - flat
    slot = jnp.sum(before * flat, axis=1, dtype=jnp.int32).reshape(routes.shape)
    target = routes * most + slot
    columns = jnp.arange(experts * most, dtype=jnp.int32)
    hits = target[:, :, None] == columns[None, None, :]
    dispatch = jnp.any(hits, axis=1).T.astype(jnp.bfloat16)
    combine = jnp.sum(jnp.where(hits, route_gate[:, :, None], 0.0), axis=1)
    return (dispatch, combine)


def shards(
    tokens,
    ssm_input,
    in_b,
    in_c,
    decay_log,
    skip_gain,
    out_proj,
    norm_gain,
    routes,
    route_gate,
    w_gate,
    w_up,
    w_down,
):
    within, state_here, cumulative, values = block_terms(ssm_input, in_b, in_c, decay_log)
    total_here = cumulative[-1]

    def link(earlier, later):
        return (earlier[0] + later[0], jnp.exp(later[0])[:, None, None] * earlier[1] + later[1])

    neutral = (jnp.zeros_like(total_here), jnp.zeros_like(state_here))
    prior = carried_in((total_here, state_here), "ctx", link, neutral)
    carried = prior[1]
    mixed = finish_heads(within, carried, cumulative, values, in_c, skip_gain)
    all_mixed = lax.all_gather(mixed, "ctx", axis=0, tiled=True)
    product = jnp.dot(all_mixed, out_proj, preferred_element_type=jnp.float32).astype(jnp.bfloat16)
    regrouped = lax.all_to_all(product, "ctx", split_axis=0, concat_axis=1, tiled=True)
    partial_out = regrouped.astype(jnp.float32)
    mixer_out = lax.psum_scatter(
        partial_out.astype(jnp.bfloat16), ("state", "expert"), scatter_dimension=1, tiled=True
    ).astype(jnp.float32)
    resid = (tokens.astype(jnp.float32) + mixer_out).astype(jnp.bfloat16)
    wide = resid.astype(jnp.float32)
    squares = lax.psum(jnp.sum(wide * wide, axis=1), ("state", "expert"))
    scale = lax.rsqrt(squares / D + norm_epsilon)
    normed = (wide * scale[:, None] * norm_gain[None, :]).astype(jnp.bfloat16)
    local_experts = w_gate.shape[0]
    experts = local_experts * lax.axis_size("expert")
    ctx_count = lax.axis_size("ctx")
    state_count = lax.axis_size("state")
    hidden_width = w_gate.shape[2]
    dispatch, combine = route_tables(routes, route_gate, experts, MOST)
    outgoing = jnp.dot(dispatch, normed, preferred_element_type=jnp.float32).astype(jnp.bfloat16)
    outgoing = outgoing.reshape(experts, MOST, normed.shape[1])
    arrived = lax.all_to_all(outgoing, "expert", split_axis=0, concat_axis=2, tiled=True)
    quarter = arrived.shape[2]
    rows = lax.all_gather(arrived, ("ctx", "state"), axis=1, tiled=True)
    rows = rows.reshape(local_experts, ctx_count, state_count, MOST, quarter)
    gate_parts = w_gate.reshape(local_experts, state_count, quarter, hidden_width)
    up_parts = w_up.reshape(local_experts, state_count, quarter, hidden_width)
    gate_value = jnp.einsum(
        "ecsrd,esdh->ecrh", rows, gate_parts, preferred_element_type=jnp.float32
    )
    up_value = jnp.einsum("ecsrd,esdh->ecrh", rows, up_parts, preferred_element_type=jnp.float32)
    hidden = (jax.nn.silu(gate_value) * up_value).astype(jnp.bfloat16)
    down_parts = w_down.reshape(local_experts, hidden_width, state_count, quarter)
    terms = jnp.einsum("ecrh,ehsd->ecsrd", hidden, down_parts, preferred_element_type=jnp.float32)
    terms = terms.reshape(local_experts, ctx_count * state_count * MOST, quarter)
    expert_out = lax.psum_scatter(
        terms.astype(jnp.bfloat16), ("ctx", "state"), scatter_dimension=1, tiled=True
    )
    returned = lax.all_to_all(expert_out, "expert", split_axis=2, concat_axis=0, tiled=True)
    returned = returned.reshape(experts * MOST, returned.shape[2])
    combined = jnp.dot(combine, returned.astype(jnp.float32), precision=lax.Precision.HIGHEST)
    return (wide + combined).astype(jnp.bfloat16)


def solution(mesh):
    in_specs = (
        P("ctx", ("state", "expert")),
        P("ctx", ("state", "expert")),
        P("ctx", None),
        P("ctx", None),
        P("ctx", ("state", "expert")),
        P(("state", "expert")),
        P(("state", "expert"), "ctx"),
        P(("state", "expert")),
        P("ctx", None),
        P("ctx", None),
        P("expert", None, ("ctx", "state")),
        P("expert", None, ("ctx", "state")),
        P("expert", ("ctx", "state"), None),
    )
    out_specs = P("ctx", ("state", "expert"))
    return jax.shard_map(shards, mesh=mesh, in_specs=in_specs, out_specs=out_specs, check_vma=False)
```

profile of v0, /device:TPU:0, one launch (start us, length us, event | category | flops | bytes accessed | tf_op | source)
XLA Modules:
  0.0 512.0 jit_solution(14820727134696495200)
XLA Ops:
  6.5 0.8 copy.174
  7.4 0.2 reduce_window_sum.26
  7.5 0.1 copy.175
  7.7 1.1 copy.177
  8.8 0.1 copy.181
  8.9 0.7 negate_sqrt_fusion
  9.7 0.7 fusion.13
  10.4 0.1 copy.183
  10.6 10.0 %all-gather = bf16[8,128,256]{2,1,0:T(8,128)(2,1)S(1)} all-gather(bf16[4,128,256]{2,1,0:T(8,128)(2,1)S(1)} %copy.183), channel_id=2, replica_groups=mesh['ctx'=2,'state'=4,'expert'=4] {'ctx'}, dimensions={0}, use_global_device_ids=true | all-gather | bytes 786432 | tf_op jit(solution)/shard_map/all_gather | solution.py:16
  20.5 4.2 all-gather.1
  24.8 0.1 copy.179
  24.9 0.1 fusion.41
  25.0 0.4 fusion.11
  25.5 0.4 fusion.12
  25.9 0.2 copy.186
  26.1 7.1 %all_gather.19 = bf16[256,1024]{0,1:T(8,128)(2,1)S(1)} all-gather(bf16[128,1024]{0,1:T(8,128)(2,1)S(1)} %bitcast.139), channel_id=1, replica_groups=mesh['ctx'=2,'state'=4,'expert'=4] {'ctx'}, dimensions={0}, use_global_device_ids=true | all-gather | bytes 786432 | tf_op jit(solution)/shard_map/all_gather | solution.py:101
  33.2 5.8 %convolution_convert_fusion = bf16[256,4096]{1,0:T(8,128)(2,1)S(1)} fusion(bf16[256,1024]{0,1:T(8,128)(2,1)S(1)} %all_gather.19, bf16[1024,4096]{1,0:T(8,128)(2,1)} %param.21), kind=kOutput, calls=%fused_computation.5 | convolution fusion | flops 2148532224 | bytes 11010048 | tf_op jit(solution)/shard_map/dot_general | solution.py:102
  39.0 0.0 copy-start.7
  39.0 24.9 %all_to_all.52 = bf16[2,128,4096]{2,1,0:T(8,128)(2,1)S(1)} all-to-all(bf16[2,128,4096]{2,1,0:T(8,128)(2,1)S(1)} %bitcast.123), channel_id=1, replica_groups=mesh['ctx'=2,'state'=4,'expert'=4] {'ctx'}, dimensions={0} | all-to-all | bytes 4194304 | tf_op jit(solution)/shard_map/all_to_all | solution.py:103
  63.9 1.5 copy.207
  65.4 0.0 reduce-scatter.2.cloned.1.call-update
  65.4 0.0 all-gather.4.cloned.1.call-start
  65.5 0.1 copy.188
  65.6 0.1 eq.43
  65.7 0.1 eq.39
  65.9 1.2 reduce-window.6
  67.1 0.1 slice.14
  67.2 0.1 copy.190
  67.3 0.1 copy.191
  67.4 0.1 add_bitcast_fusion
  67.5 0.1 reshape.122
  67.7 0.1 copy.192
  67.7 0.1 fusion.15
  67.8 59.8 %reduce-scatter.2.cloned.1.call-done = bf16[128,512]{1,0:T(8,128)(2,1)} async-done(((bf16[128,8192]{1,0:T(8,128)(2,1)}), bf16[128,512]{1,0:T(8,128)(2,1)}) %reduce-scatter.2.cloned.1.call-update) | async-done | bytes 131088 | tf_op jit(solution)/shard_map/reduce_scatter | solution.py:105
  127.6 1.0 fusion.16
  128.6 29.5 %psum.7 = f32[128]{0:T(128)S(1)} all-reduce(f32[128]{0:T(128)S(1)} %fusion.16), channel_id=1, replica_groups=mesh['ctx'=2,'state'=4,'expert'=4] {'state','expert'}, use_global_device_ids=true, to_apply=%region_10.11 | all-reduce | flops 128 | bytes 1024 | tf_op jit(solution)/shard_map/psum | solution.py:110
  158.1 1.2 convolution_convert_fusion.1
  159.4 9.1 %all_to_all.53 = bf16[4,80,512]{2,1,0:T(8,128)(2,1)S(1)} all-to-all(bf16[4,80,512]{2,1,0:T(8,128)(2,1)S(1)} %bitcast.136), channel_id=1, replica_groups=mesh['ctx'=2,'state'=4,'expert'=4] {'expert'}, dimensions={0} | all-to-all | bytes 655360 | tf_op jit(solution)/shard_map/all_to_all | solution.py:121
  168.5 0.8 copy.208
  169.2 0.0 all-gather.4.cloned.1.call-update
  169.2 0.0 all-reduce.3.cloned.1.call-start
  169.3 41.3 %reshape.127 = bf16[1536,4,2048]{2,1,0:T(4,128)(2,1)} reshape(bf16[1,1536,8192]{2,1,0:T(8,128)(2,1)} %param.27) | data formatting | bytes 50331648 | tf_op jit(solution)/shard_map/reshape.22
  210.6 10.4 %all-gather.4.cloned.1.call-done = bf16[1,640,2048]{2,1,0:T(8,128)(2,1)} async-done(((bf16[1,80,2048]{2,1,0:T(8,128)(2,1)}), bf16[1,640,2048]{2,1,0:T(8,128)(2,1)}) %all-gather.4.cloned.1.call-update) | async-done | bytes 2621456 | tf_op jit(solution)/shard_map/all_gather | solution.py:123
  221.0 13.4 %convolution_bitcast_fusion.1 = f32[2,80,1536]{2,1,0:T(8,128)S(1)} fusion(bf16[2,4,80,2048]{3,2,1,0:T(8,128)(2,1)} %bitcast.129, bf16[4,2048,1536,1]{2,1,0,3:T(8,128)(2,1)} %bitcast.122), kind=kOutput, calls=%fused_computation.9 | convolution fusion | flops 4026531840 | bytes 28770304 | tf_op jit(solution)/shard_map/ecsrd,esdh->ecrh/dot_general | solution.py:127
  234.4 10.7 %fusion.8 = bf16[2,80,1536,1]{2,1,3,0:T(8,128)(2,1)S(1)} fusion(bf16[2,4,80,2048]{3,2,1,0:T(8,128)(2,1)S(1)} %bitcast.130, bf16[4,2048,1536,1]{2,1,0,3:T(8,128)(2,1)} %bitcast.141, f32[2,80,1536]{2,1,0:T(8,128)S(1)} %convolution_bitcast_fusion.1), kind=kOutput, calls=%fused_computation.11 | convolution fusion | flops 4028006400 | bytes 29261824 | tf_op jit(solution)/shard_map/ecsrd,esdh->ecrh/dot_general | solution.py:130
  245.1 39.4 %fusion.3 = bf16[2,80,4,2048]{3,1,2,0:T(8,128)(2,1)S(1)} fusion(bf16[2,80,1536,1]{2,1,3,0:T(8,128)(2,1)S(1)} %fusion.8, bf16[1536,4,2048]{2,1,0:T(4,128)(2,1)} %reshape.127), kind=kOutput, calls=%fused_computation.6 | convolution fusion | flops 4027842560 | bytes 28278784 | tf_op jit(solution)/shard_map/ecrh,ehsd->ecsrd/dot_general | solution.py:133
  284.5 0.0 copy-start.10
  284.5 0.0 copy-start.8
  284.5 6.4 %copy.195 = bf16[1,640,2048]{2,0,1:T(2,128)(2,1)} copy(bf16[1,640,2048]{2,1,0:T(8,128)(2,1)S(1)} %bitcast.131) | data formatting | bytes 5242880 | tf_op jit(solution)/shard_map/convert_element_type | solution.py:136
  290.9 0.0 all-reduce.3.cloned.1.call-update
  290.9 0.6 dynamic-slice
  292.2 181.2 %all-reduce.3.cloned.1.call-done = bf16[1,640,2048]{2,0,1:T(2,128)(2,1)} async-done(((bf16[1,640,2048]{2,0,1:T(2,128)(2,1)}), bf16[1,640,2048]{2,0,1:T(2,128)(2,1)}) %all-reduce.3.cloned.1.call-update) | async-done | bytes 2621456
  473.4 1.8 constant_dynamic-slice_fusion
  475.2 3.0 copy.196
  478.2 0.5 broadcast.37
  478.7 11.5 %reduce = bf16[2048,80]{1,0:T(8,128)(2,1)S(1)} reduce(bf16[2048,1,80]{2,1,0:T(2,128)(2,1)S(1)} %bitcast.128, bf16[]{:T(256)} %broadcast.37), dimensions={1}, to_apply=%bitcast.101.reduce_sub_computation | reduce | bytes 655362
  490.2 1.7 reshape.142
  492.0 3.5 all-to-all-start.2
  495.5 6.6 %all-to-all-done.2 = bf16[4,2,20480]{2,1,0:T(2,128)(2,1)S(1)} async-done(((bf16[4,2,20480]{2,1,0:T(2,128)(2,1)}), bf16[4,2,20480]{2,1,0:T(2,128)(2,1)S(1)}, u32[]{:S(2)}, u32[]{:S(2)}) %all-to-all-start.2) | async-done | bytes 327712 | tf_op jit(solution)/shard_map/all_to_all | solution.py:138
  502.1 1.1 reshape.143
  503.3 0.6 copy.197
  503.9 0.2 all_to_all.47
  504.1 0.1 copy.198
  504.2 1.1 fusion.14
  (34 shorter events, 0.3 us)
Async XLA Ops:
  6.5 3.2 copy-start
  6.5 18.4 %copy-start.5 = (bf16[128,128]{1,0:T(8,128)(2,1)S(1)}, bf16[128,128]{1,0:T(8,128)(2,1)}, u32[]{:S(2)}) copy-start(bf16[128,128]{1,0:T(8,128)(2,1)} %param.18) | copy-start | bytes 98308
  6.5 18.9 %copy-start.9 = (f32[4]{0:T(128)S(1)}, f32[4]{0:T(128)}, u32[]{:S(2)}) copy-start(f32[4]{0:T(128)} %param.20) | copy-start | bytes 52
  6.5 121.1 %reduce-scatter.2.cloned.1.call-start = ((), (), s32[]{:S(2)}) async-start(), calls=%async_computation.4 | async-start | bytes 2228224 | tf_op jit(solution)/shard_map/reduce_scatter | solution.py:105
  39.0 26.5 %copy-start.6 = (s32[128,2]{0,1:T(2,128)S(1)}, s32[128,2]{0,1:T(2,128)}, u32[]{:S(2)}) copy-start(s32[128,2]{0,1:T(2,128)} %param.23) | copy-start | bytes 3076
  39.0 88.7 %copy-start.3 = (bf16[128,512]{1,0:T(8,128)(2,1)S(1)}, bf16[128,512]{1,0:T(8,128)(2,1)}, u32[]{:S(2)}) copy-start(bf16[128,512]{1,0:T(8,128)(2,1)} %param.15) | copy-start | bytes 393220
  39.0 119.2 %copy-start.7 = (f32[512]{0:T(512)S(1)}, f32[512]{0:T(512)}, u32[]{:S(2)}) copy-start(f32[512]{0:T(512)} %param.22) | copy-start | bytes 6148
  65.4 155.6 %all-gather.4.cloned.1.call-start = ((), (), s32[]{:S(2)}) async-start(), calls=%async_computation.5 | async-start | bytes 2949120 | tf_op jit(solution)/shard_map/all_gather | solution.py:123
  169.2 304.2 %all-reduce.3.cloned.1.call-start = ((), (), s32[]{:S(2)}) async-start(), calls=%async_computation.6 | async-start | bytes 10485760
  221.0 13.4 %copy-start.2 = (bf16[1,640,2048]{2,1,0:T(8,128)(2,1)S(1)}, bf16[1,640,2048]{2,1,0:T(8,128)(2,1)}, u32[]{:S(2)}) copy-start(bf16[1,640,2048]{2,1,0:T(8,128)(2,1)} %all-gather.4.cloned.1.call-done) | copy-start | bytes 7864324
  284.5 6.5 %copy-start.10 = (u32[32]{0:T(128)S(1)}, u32[32]{0:T(128)}, u32[]{:S(2)}) copy-start(u32[32]{0:T(128)} %constant.56) | copy-start | bytes 388
  284.5 210.9 %copy-start.8 = (f32[128,2]{0,1:T(2,128)S(1)}, f32[128,2]{0,1:T(2,128)}, u32[]{:S(2)}) copy-start(f32[128,2]{0,1:T(2,128)} %param.24) | copy-start | bytes 3076
  284.5 220.8 %copy-start.1 = (bf16[128,128]{1,0:T(8,128)(2,1)S(1)}, bf16[128,128]{1,0:T(8,128)(2,1)}, u32[]{:S(2)}) copy-start(bf16[128,128]{1,0:T(8,128)(2,1)} %param.17) | copy-start | bytes 98308
  290.9 213.3 %copy-start.4 = (bf16[128,512]{1,0:T(8,128)(2,1)S(1)}, bf16[128,512]{1,0:T(8,128)(2,1)}, u32[]{:S(2)}) copy-start(bf16[128,512]{1,0:T(8,128)(2,1)} %reduce-scatter.2.cloned.1.call-done) | copy-start | bytes 393220
  492.0 10.1 %all-to-all-start.2 = ((bf16[4,2,20480]{2,1,0:T(2,128)(2,1)}), bf16[4,2,20480]{2,1,0:T(2,128)(2,1)S(1)}, u32[]{:S(2)}, u32[]{:S(2)}) async-start(bf16[4,2,20480]{2,1,0:T(2,128)(2,1)} %reshape.142), calls=%async_computation.3 | async-start | bytes 655360 | tf_op jit(solution)/shard_map/all_to_all | solution.py:138
Sparse Core Ops, SparseCore 0:
  65.5 62.0 reduce-scatter.1
  169.4 51.6 all-gather.3
  291.0 182.3 all-reduce.2
where the time goes:
time: 517 us; the launch traced here: 512 us
  waiting for transfers between devices  258 us (50%)
  blocking collectives  84.7 us (16%)
  matrix products  73.2 us (14%)
  local copies, waits for them, and re-layouts  63.1 us (12%)
  other arithmetic  15 us (3%)
  between operations  14.3 us (3%)
    unnamed x4, waiting for transfers between devices  181 us
    reduce_scatter x1, waiting for transfers between devices, shards(): lax.psum_scatter(partial_out.astype(jnp.bfloat16), ('state', 'expert'), s...  59.8 us
    another operation x3, local copies, waits for them, and re-layouts  41.4 us
    dot_general x1, matrix products, shards(): jnp.einsum('ecrh,ehsd->ecsrd', hidden, down_parts, preferred_element_type...  39.4 us
    psum x1, blocking collectives, shards(): squares = lax.psum(jnp.sum(wide * wide, axis=1), ('state', 'expert'))  29.5 us
    all_to_all x1, blocking collectives, shards(): lax.all_to_all(product, 'ctx', split_axis=0, concat_axis=1, tiled=True)  24.9 us
    all_gather x2, blocking collectives, carried_in(): lax.all_gather(a.astype(kind), axis)  14.2 us
    dot_general x1, matrix products, shards(): jnp.einsum('ecsrd,esdh->ecrh', rows, gate_parts, preferred_element_type=j...  13.4 us
  transfers between devices with their start and end apart: 4, of which 4 were waited for; matrix products, arithmetic and copies ran while one was open for 9% of the time, Pallas kernels for 0%

commit v1 on v0

v1 whole, which is shorter than its diff:
```python
import functools
import math

import jax
import jax.numpy as jnp
from jax import lax
from jax.experimental import pallas as pl
from jax.experimental.pallas import tpu as pltpu
from jax.sharding import PartitionSpec as P

MOST = 80
norm_epsilon = 1e-05
MESH = pl.DeviceIdType.MESH
HIGHEST = lax.Precision.HIGHEST
VMEM_SPEC = pl.BlockSpec(memory_space=pltpu.VMEM)


def digits_of(axis, size):
    if size > 2 and size % 2 == 0 and axis == "expert":
        return [(axis, 1, 2), (axis, 2, size // 2)]
    return [(axis, 1, size)]


def value_of(digit):
    axis, stride, size = digit
    return lax.rem(lax.axis_index(axis) // stride, size)


def peer_of(digit, step):
    axis, stride, size = digit
    mine = value_of(digit)
    other = lax.rem(mine + step, size)
    return other, {axis: lax.axis_index(axis) + (other - mine) * stride}


def greet(digits):
    barrier = pltpu.get_barrier_semaphore()
    count = 0
    for digit in digits:
        for step in range(1, digit[2]):
            pl.semaphore_signal(barrier, inc=1, device_id=peer_of(digit, step)[1], device_id_type=MESH)
            count += 1
    pl.semaphore_wait(barrier, count)


def gather_kernel(jobs, used, count, *refs):
    ins, outs = refs[:count], refs[count : 2 * count]
    local_sem, send_sem, recv_sem = refs[2 * count :]
    greet(used)
    locals_ = []
    for i in range(count):
        dims = next(job[1] for job in jobs if job[0] == i)
        place = tuple(value_of(d) for d in dims)
        copy = pltpu.make_async_copy(ins[i], outs[i].at[place], local_sem.at[i])
        copy.start()
        locals_.append(copy)
    number = 0
    stages = max(len(job[2]) for job in jobs)
    sends, waiting = [], {}
    for stage in range(stages):
        for j, (i, dims, order, columns) in enumerate(jobs):
            for copy in waiting.pop(j, ()):
                copy.wait_recv()
            if stage >= len(order):
                continue
            digit = order[stage]
            done = order[:stage]
            tail = (slice(None), pl.ds(*columns))
            place = tuple(slice(None) if d in done else value_of(d) for d in dims) + tail
            copies = []
            for step in range(1, digit[2]):
                copy = pltpu.make_async_remote_copy(
                    src_ref=ins[i].at[tail] if stage == 0 else outs[i].at[place],
                    dst_ref=outs[i].at[place],
                    send_sem=send_sem.at[number],
                    recv_sem=recv_sem.at[number],
                    device_id=peer_of(digit, step)[1],
                    device_id_type=MESH,
                )
                copy.start()
                number += 1
                copies.append(copy)
            waiting[j] = copies
            sends += copies
        if stage == 0:
            for copy in locals_:
                copy.wait()
    for copies in waiting.values():
        for copy in copies:
            copy.wait_recv()
    for copy in sends:
        copy.wait_send()


def gather(arrays, jobs, ident):
    used, total = [], 0
    for _, _, order, _ in jobs:
        for digit in order:
            total += digit[2] - 1
            if digit not in used:
                used.append(digit)
    outs = []
    for i, array in enumerate(arrays):
        dims = next(job[1] for job in jobs if job[0] == i)
        outs.append(jax.ShapeDtypeStruct(tuple(d[2] for d in dims) + array.shape, array.dtype))
    return pl.pallas_call(
        functools.partial(gather_kernel, jobs, used, len(arrays)),
        out_shape=outs,
        in_specs=[VMEM_SPEC] * len(arrays),
        out_specs=[VMEM_SPEC] * len(arrays),
        scratch_shapes=[
            pltpu.SemaphoreType.DMA((len(arrays),)),
            pltpu.SemaphoreType.DMA((total,)),
            pltpu.SemaphoreType.DMA((total,)),
        ],
        compiler_params=pltpu.CompilerParams(
            collective_id=ident, has_side_effects=True, vmem_limit_bytes=56 << 20
        ),
        name=f"gather{ident}",
    )(*arrays)


def scatter_kernel(dims, parts, x_ref, out_ref, *refs):
    send_sem, recv_sem = refs[-2:]
    buffers = refs[:-2]
    greet(dims)
    number = 0
    stages = len(dims)
    sends, state = [], []
    cursor = 0
    for order, r0, rows, c0, columns in parts:
        state.append([x_ref, list(dims), (pl.ds(r0, rows), pl.ds(c0, columns)), cursor])
        cursor += 2 * stages - 1
    for stage in range(stages):
        pending = []
        for p, (order, r0, rows, c0, columns) in enumerate(parts):
            source, left, tail, base = state[p]
            digit = order[stage]
            at = left.index(digit)
            landing = buffers[base + 2 * stage]
            copies = []
            for step in range(1, digit[2]):
                other, target = peer_of(digit, step)
                place = tuple(other if k == at else slice(None) for k in range(len(left))) + tail
                copy = pltpu.make_async_remote_copy(
                    src_ref=source.at[place],
                    dst_ref=landing.at[step - 1],
                    send_sem=send_sem.at[number],
                    recv_sem=recv_sem.at[number],
                    device_id=target,
                    device_id_type=MESH,
                )
                copy.start()
                number += 1
                copies.append(copy)
            sends += copies
            pending.append(copies)
        for p, (order, r0, rows, c0, columns) in enumerate(parts):
            source, left, tail, base = state[p]
            digit = order[stage]
            at = left.index(digit)
            landing = buffers[base + 2 * stage]
            rest = left[:at] + left[at + 1 :]
            last = stage == stages - 1
            target = out_ref if last else buffers[base + 2 * stage + 1]
            mine = value_of(digit)
            for copy in pending[p]:
                copy.wait_recv()
            lead = [d[2] for d in rest]

            def add(index, _, source=source, landing=landing, target=target, lead=lead, at=at, mine=mine, tail=tail, last=last, size=digit[2]):
                where, scale = [], math.prod(lead)
                for n in lead:
                    scale //= n
                    where.append((index // scale) % n)
                where = tuple(where)
                total = source[where[:at] + (mine,) + where[at:] + tail].astype(jnp.float32)
                for k in range(size - 1):
                    total = total + landing[(k,) + where].astype(jnp.float32)
                if last:
                    target[tail_out] = total
                else:
                    target[where] = total.astype(target.dtype)
                return 0

            tail_out = (pl.ds(r0, rows), pl.ds(c0, columns))
            count = math.prod(lead)
            if count == 1:
                add(0, 0)
            else:
                lax.fori_loop(0, count, add, 0)
            state[p] = [target, rest, (slice(None), slice(None)), base]
    for copy in sends:
        copy.wait_send()


def scatter(x, dims, parts, ident):
    scratch, total = [], 0
    for order, r0, rows, c0, columns in parts:
        left = list(dims)
        for stage, digit in enumerate(order):
            left.remove(digit)
            rest = tuple(d[2] for d in left) + (rows, columns)
            scratch.append(pltpu.VMEM((digit[2] - 1,) + rest, x.dtype))
            total += digit[2] - 1
            if stage < len(order) - 1:
                scratch.append(pltpu.VMEM(rest, x.dtype))
    return pl.pallas_call(
        functools.partial(scatter_kernel, dims, parts),
        out_shape=jax.ShapeDtypeStruct(x.shape[len(dims) :], jnp.float32),
        in_specs=[VMEM_SPEC],
        out_specs=VMEM_SPEC,
        scratch_shapes=scratch
        + [pltpu.SemaphoreType.DMA((total,)), pltpu.SemaphoreType.DMA((total,))],
        compiler_params=pltpu.CompilerParams(
            collective_id=ident, has_side_effects=True, vmem_limit_bytes=56 << 20
        ),
        name=f"scatter{ident}",
    )(x)


def thirds(total, unit):
    first = max(unit, (total * 3 // 8) // unit * unit)
    return [(0, first), (first, first), (2 * first, total - 2 * first)]


def block_terms(ssm_input, in_b, in_c, decay_log):
    length = decay_log.shape[0]
    heads_here = decay_log.shape[1]
    width = ssm_input.shape[1] // heads_here
    values = ssm_input.astype(jnp.float32).reshape(length, heads_here, width)
    cumulative = jnp.cumsum(decay_log, axis=0)
    inflow = jnp.sqrt(-jnp.expm1(2.0 * decay_log))
    intersection = jnp.dot(in_c, in_b.T, preferred_element_type=jnp.float32)
    causal = jnp.arange(length)[:, None] >= jnp.arange(length)[None, :]
    spread = cumulative[:, None, :] - cumulative[None, :, :]
    fading = jnp.where(causal[:, :, None], jnp.exp(jnp.minimum(spread, 0.0)), 0.0)
    mixing = intersection[:, :, None] * fading * inflow[None, :, :]
    within = jnp.einsum("tsh,shp->thp", mixing, values, precision=HIGHEST)
    tail = jnp.exp(cumulative[-1][None, :] - cumulative) * inflow
    state_here = jnp.einsum(
        "sn,sh,shp->hnp", in_b.astype(jnp.float32), tail, values, precision=HIGHEST
    )
    return (within, state_here, cumulative, values)


def finish_heads(within, carried, cumulative, values, in_c, skip_gain):
    result = within + skip_gain[None, :, None] * values
    if carried is not None:
        outer = jnp.einsum("tn,hnp->thp", in_c.astype(jnp.float32), carried, precision=HIGHEST)
        result = result + jnp.exp(cumulative)[:, :, None] * outer
    return result.reshape(result.shape[0], -1).astype(jnp.bfloat16)


def shards(
    tokens,
    ssm_input,
    in_b,
    in_c,
    decay_log,
    skip_gain,
    out_proj,
    norm_gain,
    routes,
    route_gate,
    w_gate,
    w_up,
    w_down,
):
    n_ctx, n_state, n_expert = (lax.axis_size(a) for a in ("ctx", "state", "expert"))
    ctx_at, state_at, expert_at = (lax.axis_index(a) for a in ("ctx", "state", "expert"))
    length, block = tokens.shape
    count = n_ctx * length
    groups = n_state * n_expert
    half = out_proj.shape[1]
    width = half * n_ctx
    ctx = digits_of("ctx", n_ctx)
    state = digits_of("state", n_state)
    expert = digits_of("expert", n_expert)
    expert_down = expert[::-1]

    raw = [ssm_input, in_b, in_c, decay_log, tokens, routes, route_gate, norm_gain[None, :]]
    jobs = [(i, ctx, ctx, (0, a.shape[1])) for i, a in enumerate(raw[:-1])]
    jobs.append((len(raw) - 1, state + expert_down, state + expert_down, (0, block)))
    all_ssm, all_b, all_c, all_decay, all_tokens, all_routes, all_gate, gain = gather(raw, jobs, 0)
    gain = gain.reshape(n_ctx, 1, half)

    carried, mixed = None, []
    for c in range(n_ctx):
        within, state_here, cumulative, values = block_terms(
            all_ssm[c], all_b[c], all_c[c], all_decay[c]
        )
        mixed.append(finish_heads(within, carried, cumulative, values, all_c[c], skip_gain))
        if carried is None:
            carried = state_here
        else:
            carried = jnp.exp(cumulative[-1])[:, None, None] * carried + state_here
    all_mixed = jnp.concatenate(mixed, axis=0)

    product = jnp.dot(all_mixed, out_proj, preferred_element_type=jnp.float32)
    columns_here = half // block
    own = state_at * n_expert + expert_at - ctx_at * columns_here
    mine = (jnp.arange(columns_here, dtype=jnp.int32) == own)[:, None, None]
    token_rows = all_tokens.reshape(count, block).astype(jnp.float32)
    added = jnp.where(jnp.repeat(jnp.arange(columns_here, dtype=jnp.int32) == own, block)[None, :],
                      jnp.tile(token_rows, (1, columns_here)), 0.0)
    summands = (product + added).astype(jnp.bfloat16)
    rows = count // groups
    dims = state + expert_down
    summands = summands.reshape(tuple(d[2] for d in dims) + (rows, half))
    side = expert[1:]
    orders = [expert + state, expert[:1] + state + side]
    parts = [(order, 0, rows, k * (half // 2), half // 2) for k, order in enumerate(orders)]
    resid_piece = scatter(summands, dims, parts, 1).astype(jnp.bfloat16)

    whole = ctx + dims
    core = expert[:1]
    orders = [state + ctx + side + core, state + side + ctx + core, side + ctx + state + core]
    jobs = [(0, whole, order, cut) for order, cut in zip(orders, thirds(half, 128))]
    (resid,) = gather([resid_piece], jobs, 2)
    resid = resid.reshape(n_ctx, count, half)

    wide = resid.astype(jnp.float32)
    scale = lax.rsqrt(jnp.sum(wide * wide, axis=(0, 2)) / width + norm_epsilon)

    routed = all_routes == expert_at
    chosen = jnp.any(routed, axis=2)
    weight = jnp.sum(jnp.where(routed, all_gate, 0.0), axis=2).reshape(count)
    flags = chosen.astype(jnp.bfloat16)
    earlier = (jnp.arange(length)[:, None] < jnp.arange(length)[None, :]).astype(jnp.bfloat16)
    slot = jnp.dot(flags, earlier, preferred_element_type=jnp.float32).astype(jnp.int32)
    target = jnp.where(chosen, slot + MOST * jnp.arange(n_ctx, dtype=jnp.int32)[:, None], -1)
    hits = jnp.arange(n_ctx * MOST, dtype=jnp.int32)[:, None] == target.reshape(1, count)
    dispatch = hits.astype(jnp.bfloat16)
    slot_weight = jnp.sum(jnp.where(hits, weight[None, :], 0.0), axis=1)
    slot_scale = jnp.sum(jnp.where(hits, scale[None, :], 0.0), axis=1)

    picked = jnp.einsum("rt,ctd->crd", dispatch, resid, preferred_element_type=jnp.float32)
    entering = (picked * slot_scale[None, :, None] * gain).astype(jnp.bfloat16)
    gate_parts = w_gate.reshape(n_ctx, half, w_gate.shape[2])
    up_parts = w_up.reshape(n_ctx, half, w_up.shape[2])
    gate_value = jnp.einsum("crd,cdh->rh", entering, gate_parts, preferred_element_type=jnp.float32)
    up_value = jnp.einsum("crd,cdh->rh", entering, up_parts, preferred_element_type=jnp.float32)
    hidden = (jax.nn.silu(gate_value) * up_value * slot_weight[:, None]).astype(jnp.bfloat16)
    terms = jnp.dot(hidden, w_down[0], preferred_element_type=jnp.float32).astype(jnp.bfloat16)
    spread = jnp.einsum(
        "rt,rgd->gtd", dispatch, terms.reshape(-1, groups, block), preferred_element_type=jnp.float32
    ).astype(jnp.bfloat16)
    dims = state + expert_down + ctx
    spread = spread.reshape(tuple(d[2] for d in dims) + (length, block))
    orders = [core + side + ctx + state, core + ctx + side + state, core + state + side + ctx]
    parts = [(order, r0, n, 0, block) for order, (r0, n) in zip(orders, thirds(length, 16))]
    combined = scatter(spread, dims, parts, 3)

    position = (state_at * n_expert + expert_at) * block
    own_resid = lax.dynamic_slice(
        resid, (position // half, ctx_at * length, position % half), (1, length, block)
    )[0]
    return (own_resid.astype(jnp.float32) + combined).astype(jnp.bfloat16)


def solution(mesh):
    in_specs = (
        P("ctx", ("state", "expert")),
        P("ctx", ("state", "expert")),
        P("ctx", None),
        P("ctx", None),
        P("ctx", ("state", "expert")),
        P(("state", "expert")),
        P(("state", "expert"), "ctx"),
        P(("state", "expert")),
        P("ctx", None),
        P("ctx", None),
        P("expert", None, ("ctx", "state")),
        P("expert", None, ("ctx", "state")),
        P("expert", ("ctx", "state"), None),
    )
    out_specs = P("ctx", ("state", "expert"))
    return jax.shard_map(shards, mesh=mesh, in_specs=in_specs, out_specs=out_specs, check_vma=False)
```

time: 517 us -> 197 us (0.38)
  waiting for transfers between devices: 258 us -> 0 us
  Pallas kernels: 0 us -> 126 us
  blocking collectives: 84.7 us -> 0 us
  local copies, waits for them, and re-layouts: 63.1 us -> 10.7 us
  matrix products: 73.2 us -> 50.3 us
  between operations: 14.3 us -> 0.31 us
  other arithmetic: 15 us -> 9.27 us
    unnamed x4 -> x0, waiting for transfers between devices: 181 us -> none
    pallas_call x0 -> x4, Pallas kernels: none -> 126 us  [the longest x2 66.2 us: scatter(): pl.pallas_call(functools.partial(scatter_kernel, dims, parts), out_shape=...]
    reduce_scatter x1 -> x0, waiting for transfers between devices: 59.8 us -> none  [shards(): lax.psum_scatter(partial_out.astype(jnp.bfloat16), ('state', 'expert'), s...]
    another operation x3 -> x1, local copies, waits for them, and re-layouts: 41.4 us -> 0.52 us  [shards(): jnp.tile(token_rows, (1, columns_here))]
    all_to_all x2 -> x0, blocking collectives: 34 us -> none  [the longest x1 24.9 us: shards(): lax.all_to_all(product, 'ctx', split_axis=0, concat_axis=1, tiled=True)]
    psum x1 -> x0, blocking collectives: 29.5 us -> none  [shards(): squares = lax.psum(jnp.sum(wide * wide, axis=1), ('state', 'expert'))]
    dot_general x8 -> x9, matrix products: 72.3 us -> 48.8 us  [the longest x1 20 us: shards(): jnp.dot(hidden, w_down[0], preferred_element_type=jnp.float32)]
    all_gather x3 -> x0, blocking collectives: 21.3 us -> none  [the longest x2 14.2 us: carried_in(): lax.all_gather(a.astype(kind), axis)]
  transfers between devices with their start and end apart: 4 -> 0, of which waited for: 4 -> 0; matrix products, arithmetic and copies ran while one was open for 9% -> 0% of each run, Pallas kernels for 0% -> 0%
where the time goes in v1:
time: 197 us
  Pallas kernels  126 us (64%)
  matrix products  50.3 us (26%)
  local copies, waits for them, and re-layouts  10.7 us (5%)
  other arithmetic  9.27 us (5%)
    pallas_call x2, Pallas kernels, scatter(): pl.pallas_call(functools.partial(scatter_kernel, dims, parts), out_shape=...  66.2 us
    pallas_call x2, Pallas kernels, gather(): pl.pallas_call(functools.partial(gather_kernel, jobs, used, len(arrays)),...  59.7 us
    dot_general x1, matrix products, shards(): jnp.dot(hidden, w_down[0], preferred_element_type=jnp.float32)  20 us
    dot_general x1, matrix products, shards(): jnp.einsum('crd,cdh->rh', entering, gate_parts, preferred_element_type=jn...  12.3 us
    unnamed x22, local copies, waits for them, and re-layouts  8.16 us
    dot_general x1, matrix products, shards(): product = jnp.dot(all_mixed, out_proj, preferred_element_type=jnp.float32)  7.45 us

profile of v1, /device:TPU:0, one launch (start us, length us, event | category | flops | bytes accessed | tf_op | source)
XLA Modules:
  0.0 196.5 jit_solution(7706909823420198564)
XLA Ops:
  0.0 0.0 copy-start.6
  0.0 1.4 copy.31.refs_3_
  1.4 1.4 copy.32.refs_5_
  2.8 1.4 copy.33.refs_6_
  4.3 28.0 %gather0.1 = (bf16[2,128,1024]{2,1,0:T(8,128)(2,1)}, bf16[2,128,128]{2,1,0:T(8,128)(2,1)}, bf16[2,128,128]{2,1,0:T(8,128)(2,1)}, f32[2,128,4]{2,1,0:T(8,128)}, b...) custom-call(bf16[128,1024]{1,0:T(8,128)(2,1)} %refs_0_.1, ...), custom_call_target="tpu_custom_call" | custom-call | tf_op jit(solution)/shard_map/gather0/pallas_call | solution.py:106
  32.2 0.0 copy-start.1
  32.2 0.0 copy-start.2
  32.2 0.0 copy-start
  32.2 1.0 sqrt_bitcast_fusion.1
  33.3 0.2 reduce_window_sum.17
  33.4 0.9 sqrt_multiply_fusion
  34.3 0.1 copy.47
  34.4 1.1 fusion.82
  35.5 0.2 copy.51
  35.7 1.2 convolution_bitcast_fusion.2
  36.9 0.2 reduce_window_sum.18
  37.1 0.1 copy.46
  37.2 1.4 convolution_multiply_fusion.1
  38.5 0.0 copy-done.1
  38.5 0.0 copy-done.2
  38.5 0.1 fusion.65
  38.7 0.1 copy.40
  38.8 0.1 copy.43
  38.8 0.2 copy.52
  39.1 0.0 copy-done.6
  39.1 0.5 fusion.17
  39.6 0.1 fusion.68
  39.7 0.1 copy.34
  39.8 0.1 copy.37
  39.9 0.5 fusion.18
  40.5 0.1 broadcast_bitcast_fusion
  40.6 0.0 copy-done
  40.6 0.1 bitcast_convert_fusion
  40.6 0.5 tile.4
  41.2 3.8 %copy.55 = f32[32,8,8,512]{3,1,2,0:T(8,128)S(1)} copy(f32[32,8,8,512]{3,2,1,0:T(8,128)S(1)} %bitcast.113) | data formatting | bytes 8388608
  45.0 7.5 %fusion.7 = bf16[256,4096]{1,0:T(8,128)(2,1)} fusion(bf16[1024,4096]{1,0:T(8,128)(2,1)} %param.19, f32[256,4096]{1,0:T(8,128)S(1)} %bitcast.111, pred[4096]{0:T(1024)(128)(4,1)S(1)} %bitcast.121, bf16[128,1024]{0,1:T(8,128)(2,1)S(1)} %bitcast.116, bf16[128,1024]{0,1:T(8,128)(2,1)S(1)} %bitcast.120), kind=kOutput, calls=%fused_computation.8 | convolution fusion | flops 2151677952 | bytes 15208448 | tf_op jit(solution)/shard_map/dot_general | solution.py:300
  52.4 25.0 %scatter1.1 = f32[16,4096]{1,0:T(8,128)} custom-call(bf16[4,2,2,16,4096]{4,3,2,1,0:T(8,128)(2,1)} %bitcast.114), custom_call_target="tpu_custom_call" | custom-call | tf_op jit(solution)/shard_map/scatter1/pallas_call | solution.py:208
  77.5 1.6 convert_element_type.84.refs_0_
  79.1 0.0 copy-start.4
  79.1 0.0 copy-start.3
  79.1 0.0 copy-start.5
  79.1 31.7 %gather2.1 = bf16[2,4,2,2,16,4096]{5,4,3,2,1,0:T(8,128)(2,1)} custom-call(bf16[16,4096]{1,0:T(8,128)(2,1)} %convert_element_type.84.refs_0_), custom_call_target="tpu_custom_call" | custom-call | tf_op jit(solution)/shard_map/gather2/pallas_call | solution.py:106
  110.8 3.1 %multiply_reduce_fusion = f32[4,2,2,16]{3,2,1,0:T(2,128)S(1)} fusion(bf16[2,4,2,2,16,4096]{5,4,3,2,1,0:T(8,128)(2,1)} %gather2.1), kind=kLoop, calls=%fused_computation.3 | loop fusion | flops 6291200 | bytes 4195328 | tf_op jit(solution)/shard_map/reduce_sum | solution.py:324
  113.9 0.1 rsqrt.11
  114.0 0.0 copy-done.4
  114.0 0.1 fusion.81
  114.1 0.0 copy-done.3
  114.1 0.1 select_reduce_fusion.2
  114.3 0.1 fusion.21
  114.4 0.2 select_reduce_fusion
  114.6 0.0 copy-done.5
  114.6 0.1 reduce.1
  114.7 3.2 %fusion.8 = bf16[2,160,4096]{2,1,0:T(8,128)(2,1)S(1)} fusion(bf16[2,256,4096]{2,1,0:T(8,128)(2,1)} %bitcast.109, f32[2,4096]{1,0:T(2,128)S(1)} %mul.158, f32[160]{0:T(256)S(1)} %get-tuple-element.22, s32[256]{0:T(256)S(1)} %fusion.21), kind=kOutput, calls=%fused_computation.9 | convolution fusion | flops 675061760 | bytes 6850176 | tf_op jit(solution)/shard_map/rt,ctd->crd/dot_general | solution.py:338
  117.9 0.0 copy-start.7
  117.9 12.3 %convolution_bitcast_fusion.1 = f32[160,1536]{1,0:T(8,128)} fusion(bf16[2,160,4096]{2,1,0:T(8,128)(2,1)S(1)} %fusion.8, bf16[2,4096,1536]{2,1,0:T(8,128)(2,1)} %bitcast.124), kind=kOutput, calls=%fused_computation.16 | convolution fusion | flops 4026531840 | bytes 28770304 | tf_op jit(solution)/shard_map/crd,cdh->rh/dot_general | solution.py:342
  130.2 0.0 copy-done.7
  130.2 20.0 %fusion.2 = bf16[160,8192]{1,0:T(8,128)(2,1)S(1)} fusion(bf16[1,1536,8192]{2,1,0:T(8,128)(2,1)} %param.25, bf16[2,160,4096]{2,1,0:T(8,128)(2,1)} %copy-done.7, bf16[2,4096,1536]{2,1,0:T(8,128)(2,1)} %bitcast.125, f32[160,1536]{1,0:T(8,128)} %convolution_bitcast_fusion.1, f32[160]{0:T(256)S(1)} %get-tuple-element.21), kind=kOutput, calls=%fused_computation.2 | convolution fusion | flops 8056094720 | bytes 56558208 | tf_op jit(solution)/shard_map/dot_general | solution.py:345
  150.2 3.4 %convolution_convert_fusion = bf16[16,512,256]{1,2,0:T(8,128)(2,1)} fusion(bf16[20,16,8,512]{3,2,1,0:T(8,128)(2,1)S(1)} %bitcast.115, s32[256]{0:T(256)S(1)} %fusion.21), kind=kOutput, calls=%fused_computation.10 | convolution fusion | flops 673226752 | bytes 6816768 | tf_op jit(solution)/shard_map/rt,rgd->gtd/dot_general | solution.py:346
  153.6 41.2 %scatter3.1 = f32[128,512]{1,0:T(8,128)} custom-call(bf16[4,2,2,2,128,512]{5,4,3,2,1,0:T(8,128)(2,1)} %bitcast.112), custom_call_target="tpu_custom_call" | custom-call | tf_op jit(solution)/shard_map/scatter3/pallas_call | solution.py:208
  194.8 1.7 fusion.32
  (8 shorter events, 0.1 us)
Async XLA Ops:
  0.0 39.1 %copy-start.6 = (f32[4]{0:T(128)S(1)}, f32[4]{0:T(128)}, u32[]{:S(2)}) copy-start(f32[4]{0:T(128)} %param.18) | copy-start | bytes 52
  32.2 6.3 %copy-start.1 = (bf16[2,128,128]{2,1,0:T(8,128)(2,1)S(1)}, bf16[2,128,128]{2,1,0:T(8,128)(2,1)}, u32[]{:S(2)}) copy-start(bf16[2,128,128]{2,1,0:T(8,128)(2,1)} %get-tuple-element.15) | copy-start | bytes 196612
  32.2 6.3 %copy-start.2 = (bf16[2,128,128]{2,1,0:T(8,128)(2,1)S(1)}, bf16[2,128,128]{2,1,0:T(8,128)(2,1)}, u32[]{:S(2)}) copy-start(bf16[2,128,128]{2,1,0:T(8,128)(2,1)} %get-tuple-element.14) | copy-start | bytes 196612
  32.2 8.3 %copy-start = (bf16[2,128,512]{2,1,0:T(8,128)(2,1)S(1)}, bf16[2,128,512]{2,1,0:T(8,128)(2,1)}, u32[]{:S(2)}) copy-start(bf16[2,128,512]{2,1,0:T(8,128)(2,1)} %get-tuple-element.17) | copy-start | bytes 786436
  79.1 34.9 %copy-start.4 = (s32[2,128,2]{2,1,0:T(8,128)S(1)}, s32[2,128,2]{2,1,0:T(8,128)}, u32[]{:S(2)}) copy-start(s32[2,128,2]{2,1,0:T(8,128)} %get-tuple-element.18) | copy-start | bytes 6148
  79.1 35.0 %copy-start.3 = (f32[2,128,2]{2,1,0:T(8,128)S(1)}, f32[2,128,2]{2,1,0:T(8,128)}, u32[]{:S(2)}) copy-start(f32[2,128,2]{2,1,0:T(8,128)} %get-tuple-element.20) | copy-start | bytes 6148
  79.1 35.5 %copy-start.5 = (f32[4,2,2,1,512]{4,3,2,1,0:T(1,128)S(1)}, f32[4,2,2,1,512]{4,3,2,1,0:T(1,128)}, u32[]{:S(2)}) copy-start(f32[4,2,2,1,512]{4,3,2,1,0:T(1,128)} %get-tuple-element.19) | copy-start | bytes 98308
  117.9 12.3 %copy-start.7 = (bf16[2,160,4096]{2,1,0:T(8,128)(2,1)}, bf16[2,160,4096]{2,1,0:T(8,128)(2,1)S(1)}, u32[]{:S(2)}) copy-start(bf16[2,160,4096]{2,1,0:T(8,128)(2,1)S(1)} %fusion.8) | copy-start | bytes 7864324

commit v2 on v1

--- a/solution.py
+++ b/solution.py
@@ -124,77 +124,77 @@
     send_sem, recv_sem = refs[-2:]
     buffers = refs[:-2]
     greet(dims)
-    number = 0
     stages = len(dims)
-    sends, state = [], []
-    cursor = 0
-    for order, r0, rows, c0, columns in parts:
-        state.append([x_ref, list(dims), (pl.ds(r0, rows), pl.ds(c0, columns)), cursor])
-        cursor += 2 * stages - 1
+    sends, pending, state = [], {}, []
+    for p, (order, r0, rows, c0, columns) in enumerate(parts):
+        tail = (pl.ds(r0, rows), pl.ds(c0, columns))
+        state.append((x_ref, list(dims), tail, p * (2 * stages - 1)))
+
+    def begin(p, stage):
+        source, left, tail, base = state[p]
+        digit = parts[p][0][stage]
+        at = left.index(digit)
+        pending[p] = []
+        for step in range(1, digit[2]):
+            other, target = peer_of(digit, step)
+            place = tuple(other if k == at else slice(None) for k in range(len(left))) + tail
+            copy = pltpu.make_async_remote_copy(
+                src_ref=source.at[place],
+                dst_ref=buffers[base + 2 * stage].at[step - 1],
+                send_sem=send_sem.at[len(sends)],
+                recv_sem=recv_sem.at[len(sends)],
+                device_id=target,
+                device_id_type=MESH,
+            )
+            copy.start()
+            sends.append(copy)
+            pending[p].append(copy)
+
+    def finish(p, stage):
+        order, r0, rows, c0, columns = parts[p]
+        source, left, tail, base = state[p]
+        digit = order[stage]
+        at = left.index(digit)
+        rest = left[:at] + left[at + 1 :]
+        landing = buffers[base + 2 * stage]
+        last = stage == stages - 1
+        target = out_ref if last else buffers[base + 2 * stage + 1]
+        mine = value_of(digit)
+        for copy in pending[p]:
+            copy.wait_recv()
+        count = math.prod(d[2] for d in rest)
+
+        def add(index, _):
+            where, scale = [], count
+            for d in rest:
+                scale //= d[2]
+                where.append((index // scale) % d[2])
+            where = tuple(where)
+            total = source[where[:at] + (mine,) + where[at:] + tail].astype(jnp.float32)
+            for k in range(digit[2] - 1):
+                total = total + landing[(k,) + where].astype(jnp.float32)
+            spot = (pl.ds(r0, rows), pl.ds(c0, columns)) if last else where
+            target[spot] = total.astype(target.dtype)
+            return 0
+
+        if count == 1:
+            add(0, 0)
+        else:
+            lax.fori_loop(0, count, add, 0)
+        state[p] = (target, rest, (slice(None), slice(None)), base)
+
+    for p in range(len(parts)):
+        begin(p, 0)
     for stage in range(stages):
-        pending = []
-        for p, (order, r0, rows, c0, columns) in enumerate(parts):
-            source, left, tail, base = state[p]
-            digit = order[stage]
-            at = left.index(digit)
-            landing = buffers[base + 2 * stage]
-            copies = []
-            for step in range(1, digit[2]):
-                other, target = peer_of(digit, step)
-                place = tuple(other if k == at else slice(None) for k in range(len(left))) + tail
-                copy = pltpu.make_async_remote_copy(
-                    src_ref=source.at[place],
-                    dst_ref=landing.at[step - 1],
-                    send_sem=send_sem.at[number],
-                    recv_sem=recv_sem.at[number],
-                    device_id=target,
-                    device_id_type=MESH,
-                )
-                copy.start()
-                number += 1
-                copies.append(copy)
-            sends += copies
-            pending.append(copies)
-        for p, (order, r0, rows, c0, columns) in enumerate(parts):
-            source, left, tail, base = state[p]
-            digit = order[stage]
-            at = left.index(digit)
-            landing = buffers[base + 2 * stage]
-            rest = left[:at] + left[at + 1 :]
-            last = stage == stages - 1
-            target = out_ref if last else buffers[base + 2 * stage + 1]
-            mine = value_of(digit)
-            for copy in pending[p]:
-                copy.wait_recv()
-            lead = [d[2] for d in rest]
-
-            def add(index, _, source=source, landing=landing, target=target, lead=lead, at=at, mine=mine, tail=tail, last=last, size=digit[2]):
-                where, scale = [], math.prod(lead)
-                for n in lead:
-                    scale //= n
-                    where.append((index // scale) % n)
-                where = tuple(where)
-                total = source[where[:at] + (mine,) + where[at:] + tail].astype(jnp.float32)
-                for k in range(size - 1):
-                    total = total + landing[(k,) + where].astype(jnp.float32)
-                if last:
-                    target[tail_out] = total
-                else:
-                    target[where] = total.astype(target.dtype)
-                return 0
-
-            tail_out = (pl.ds(r0, rows), pl.ds(c0, columns))
-            count = math.prod(lead)
-            if count == 1:
-                add(0, 0)
-            else:
-                lax.fori_loop(0, count, add, 0)
-            state[p] = [target, rest, (slice(None), slice(None)), base]
+        for p in range(len(parts)):
+            finish(p, stage)
+            if stage < stages - 1:
+                begin(p, stage + 1)
     for copy in sends:
         copy.wait_send()
 
 
-def scatter(x, dims, parts, ident):
+def scatter(x, dims, parts, ident, kind):
     scratch, total = [], 0
     for order, r0, rows, c0, columns in parts:
         left = list(dims)
@@ -207,7 +207,7 @@
                 scratch.append(pltpu.VMEM(rest, x.dtype))
     return pl.pallas_call(
         functools.partial(scatter_kernel, dims, parts),
-        out_shape=jax.ShapeDtypeStruct(x.shape[len(dims) :], jnp.float32),
+        out_shape=jax.ShapeDtypeStruct(x.shape[len(dims) :], kind),
         in_specs=[VMEM_SPEC],
         out_specs=VMEM_SPEC,
         scratch_shapes=scratch
@@ -222,6 +222,11 @@
 def thirds(total, unit):
     first = max(unit, (total * 3 // 8) // unit * unit)
     return [(0, first), (first, first), (2 * first, total - 2 * first)]
+
+
+def halves(total):
+    first = max(128, (total // 2 + 127) // 128 * 128)
+    return [(0, first), (first, total - first)]
 
 
 def block_terms(ssm_input, in_b, in_c, decay_log):
@@ -279,11 +284,14 @@
     expert = digits_of("expert", n_expert)
     expert_down = expert[::-1]
 
-    raw = [ssm_input, in_b, in_c, decay_log, tokens, routes, route_gate, norm_gain[None, :]]
-    jobs = [(i, ctx, ctx, (0, a.shape[1])) for i, a in enumerate(raw[:-1])]
-    jobs.append((len(raw) - 1, state + expert_down, state + expert_down, (0, block)))
-    all_ssm, all_b, all_c, all_decay, all_tokens, all_routes, all_gate, gain = gather(raw, jobs, 0)
-    gain = gain.reshape(n_ctx, 1, half)
+    heads, top = decay_log.shape[1], routes.shape[1]
+    small = jnp.concatenate([decay_log.T, route_gate.T, routes.T.astype(jnp.float32)], axis=0)
+    raw = [ssm_input, in_b, in_c, small, tokens]
+    jobs = [(i, ctx, ctx, (0, a.shape[1])) for i, a in enumerate(raw)]
+    all_ssm, all_b, all_c, all_small, all_tokens = gather(raw, jobs, 0)
+    all_decay = all_small[:, :heads].transpose(0, 2, 1)
+    all_gate = all_small[:, heads : heads + top].transpose(0, 2, 1)
+    all_routes = all_small[:, heads + top :].transpose(0, 2, 1).astype(jnp.int32)
 
     carried, mixed = None, []
     for c in range(n_ctx):
@@ -297,27 +305,34 @@
             carried = jnp.exp(cumulative[-1])[:, None, None] * carried + state_here
     all_mixed = jnp.concatenate(mixed, axis=0)
 
-    product = jnp.dot(all_mixed, out_proj, preferred_element_type=jnp.float32)
-    columns_here = half // block
-    own = state_at * n_expert + expert_at - ctx_at * columns_here
-    mine = (jnp.arange(columns_here, dtype=jnp.int32) == own)[:, None, None]
-    token_rows = all_tokens.reshape(count, block).astype(jnp.float32)
-    added = jnp.where(jnp.repeat(jnp.arange(columns_here, dtype=jnp.int32) == own, block)[None, :],
-                      jnp.tile(token_rows, (1, columns_here)), 0.0)
-    summands = (product + added).astype(jnp.bfloat16)
+    product = jnp.dot(all_mixed, out_proj, preferred_element_type=jnp.float32).astype(jnp.bfloat16)
+    own = (state_at * n_expert + expert_at) * block - ctx_at * half
+    held = jnp.logical_and(own >= 0, own < half)
+    start = jnp.clip(own, 0, half - block)
+    patch = lax.dynamic_slice(product, (0, start), (count, block)).astype(jnp.float32)
+    patch = patch + jnp.where(held, all_tokens.reshape(count, block).astype(jnp.float32), 0.0)
+    summands = lax.dynamic_update_slice(product, patch.astype(jnp.bfloat16), (0, start))
     rows = count // groups
     dims = state + expert_down
     summands = summands.reshape(tuple(d[2] for d in dims) + (rows, half))
     side = expert[1:]
     orders = [expert + state, expert[:1] + state + side]
-    parts = [(order, 0, rows, k * (half // 2), half // 2) for k, order in enumerate(orders)]
-    resid_piece = scatter(summands, dims, parts, 1).astype(jnp.bfloat16)
+    parts = [
+        (order, 0, rows, k * (half // 2) + start, size)
+        for start, size in halves(half // 2)
+        for k, order in enumerate(orders)
+    ]
+    resid_piece = scatter(summands, dims, parts, 1, jnp.bfloat16)
 
     whole = ctx + dims
     core = expert[:1]
     orders = [state + ctx + side + core, state + side + ctx + core, side + ctx + state + core]
-    jobs = [(0, whole, order, cut) for order, cut in zip(orders, thirds(half, 128))]
-    (resid,) = gather([resid_piece], jobs, 2)
+    cuts = [[(a + start, size) for start, size in halves(n)] for a, n in thirds(half, 128)]
+    jobs = [(0, whole, order, cut[k]) for k in range(2) for order, cut in zip(orders, cuts)]
+    spread_over = state + expert_down
+    jobs.append((1, spread_over, spread_over, (0, block)))
+    resid, gain = gather([resid_piece, norm_gain[None, :]], jobs, 2)
+    gain = gain.reshape(n_ctx, 1, half)
     resid = resid.reshape(n_ctx, count, half)
 
     wide = resid.astype(jnp.float32)
@@ -349,8 +364,12 @@
     dims = state + expert_down + ctx
     spread = spread.reshape(tuple(d[2] for d in dims) + (length, block))
     orders = [core + side + ctx + state, core + ctx + side + state, core + state + side + ctx]
-    parts = [(order, r0, n, 0, block) for order, (r0, n) in zip(orders, thirds(length, 16))]
-    combined = scatter(spread, dims, parts, 3)
+    parts = [
+        (order, r0, n, start, size)
+        for start, size in halves(block)
+        for order, (r0, n) in zip(orders, thirds(length, 16))
+    ]
+    combined = scatter(spread, dims, parts, 3, jnp.float32)
 
     position = (state_at * n_expert + expert_at) * block
     own_resid = lax.dynamic_slice(

time: 197 us -> 168 us (0.85)
  Pallas kernels: 126 us -> 104 us
  local copies, waits for them, and re-layouts: 10.7 us -> 6.64 us
    pallas_call x2, Pallas kernels: 59.7 us -> 48.3 us  [gather(): pl.pallas_call(functools.partial(gather_kernel, jobs, used, len(arrays)),...]
    pallas_call x2, Pallas kernels: 66.2 us -> 55.5 us  [scatter(): pl.pallas_call(functools.partial(scatter_kernel, dims, parts), out_shape=...]
    unnamed x22 -> x16, local copies, waits for them, and re-layouts: 8.16 us -> 1.37 us
    dynamic_update_slice x0 -> x1, local copies, waits for them, and re-layouts: none -> 2.49 us  [shards(): lax.dynamic_update_slice(product, patch.astype(jnp.bfloat16), (0, start))]
where the time goes in v2:
time: 168 us; the launch traced here: 167 us
  Pallas kernels  104 us (62%)
  matrix products  48.6 us (29%)
  other arithmetic  7.8 us (5%)
  local copies, waits for them, and re-layouts  6.64 us (4%)
    pallas_call x2, Pallas kernels, scatter(): pl.pallas_call(functools.partial(scatter_kernel, dims, parts), out_shape=...  55.5 us
    pallas_call x2, Pallas kernels, gather(): pl.pallas_call(functools.partial(gather_kernel, jobs, used, len(arrays)),...  48.3 us
    dot_general x1, matrix products, shards(): jnp.dot(hidden, w_down[0], preferred_element_type=jnp.float32)  20 us
    dot_general x1, matrix products, shards(): jnp.einsum('crd,cdh->rh', entering, gate_parts, preferred_element_type=jn...  12.3 us
    dot_general x1, matrix products, shards(): jnp.dot(all_mixed, out_proj, preferred_element_type=jnp.float32)  5.8 us
    dot_general x1, matrix products, shards(): jnp.einsum('rt,rgd->gtd', dispatch, terms.reshape(-1, groups, block), pre...  3.39 us

profile of v2, /device:TPU:0, one launch (start us, length us, event | category | flops | bytes accessed | tf_op | source)
XLA Modules:
  0.0 167.1 jit_solution(9195111275069045909)
XLA Ops:
  0.0 0.0 copy-start.6
  0.0 0.7 convert_bitcast_fusion
  0.7 1.3 pad_maximum_fusion.refs_3_
  2.0 16.0 %gather0.1 = (bf16[2,128,1024]{2,1,0:T(8,128)(2,1)}, bf16[2,128,128]{2,1,0:T(8,128)(2,1)}, bf16[2,128,128]{2,1,0:T(8,128)(2,1)}, f32[2,8,128]{2,1,0:T(8,128)}, bf16[2,128,512]{2,1,0:T(8,128)(2,1)}) custom-call(bf16[128,1024]{1,0:T(8,128)(2,1)} %refs_0_.1, bf16[128,128]{1,0:T(8,128)(2,1)} %refs_1_.1, bf16[128,128]{1,0:T(8,128)(2,1)} %refs_2_.1, ...), custom_call_target="tpu_custom_call" | custom-call | tf_op jit(solution)/shard_map/gather0/pallas_call | solution.py:106
  18.0 0.0 copy-start.2
  18.0 0.0 copy-start.3
  18.0 0.7 slice_bitcast_fusion
  18.8 0.1 copy.14
  18.9 0.2 reduce_window_sum.17
  19.1 0.1 copy.15
  19.1 0.1 sqrt_multiply_fusion
  19.2 1.1 fusion.82
  20.3 0.2 copy.29
  20.5 1.2 convolution_bitcast_fusion.2
  21.7 0.1 copy.19
  21.8 0.2 reduce_window_sum.18
  22.0 0.1 copy.24
  22.1 1.4 convolution_multiply_fusion.1
  23.4 0.0 copy-done.2
  23.4 0.0 copy-done.3
  23.5 0.1 fusion.65
  23.6 0.1 copy.20
  23.7 0.2 copy.30
  23.9 0.0 copy-done.6
  23.9 0.5 fusion.16
  24.4 0.1 fusion.68
  24.6 0.5 fusion.17
  25.1 0.0 copy-start.1
  25.1 5.8 %convolution_convert_fusion = bf16[256,4096]{1,0:T(8,128)(2,1)S(1)} fusion(bf16[1024,4096]{1,0:T(8,128)(2,1)} %param.19, bf16[128,1024]{0,1:T(8,128)(2,1)S(1)} %bitcast.126, bf16[128,1024]{0,1:T(8,128)(2,1)S(1)} %bitcast.127), kind=kOutput, calls=%fused_computation.7 | convolution fusion | flops 2149580800 | bytes 11010048 | tf_op jit(solution)/shard_map/dot_general | solution.py:308
  30.9 0.0 copy-done.1
  31.0 0.1 convert_select_fusion
  31.0 0.0 copy-start.5
  31.0 0.1 fusion.29
  31.2 2.5 %dynamic_update_slice.3 = bf16[256,4096]{1,0:T(8,128)(2,1)S(1)} dynamic-update-slice(bf16[256,4096]{1,0:T(8,128)(2,1)S(1)} %convolution_convert_fusion, bf16[256,512]{1,0:T(8,128)(2,1)S(1)} %fusion.29, s32[]{:T(128)} %constant.54.clone.1, s32[]{:T(128)S(6)} %min.12) | dynamic-update-slice | bytes 524292 | tf_op jit(solution)/shard_map/dynamic_update_slice | solution.py:314
  33.7 0.0 copy-start
  33.7 1.3 copy-done
  35.0 23.4 %scatter1.1.refs_0_ = bf16[16,4096]{1,0:T(8,128)(2,1)} custom-call(bf16[4,2,2,16,4096]{4,3,2,1,0:T(8,128)(2,1)} %bitcast.119), custom_call_target="tpu_custom_call" | custom-call | tf_op jit(solution)/shard_map/scatter1/pallas_call | solution.py:208
  58.5 32.3 %gather2.1 = (bf16[2,4,2,2,16,4096]{5,4,3,2,1,0:T(8,128)(2,1)}, f32[4,2,2,1,512]{4,3,2,1,0:T(1,128)}) custom-call(bf16[16,4096]{1,0:T(8,128)(2,1)} %scatter1.1.refs_0_, f32[1,512]{1,0:T(1,128)} %bitcast.129), custom_call_target="tpu_custom_call" | custom-call | tf_op jit(solution)/shard_map/gather2/pallas_call | solution.py:106
  90.8 0.0 copy-start.4
  90.8 3.1 %multiply_reduce_fusion = f32[4,2,2,16]{3,2,1,0:T(2,128)S(1)} fusion(bf16[2,4,2,2,16,4096]{5,4,3,2,1,0:T(8,128)(2,1)} %get-tuple-element.17), kind=kLoop, calls=%fused_computation.3 | loop fusion | flops 6291200 | bytes 4195328 | tf_op jit(solution)/shard_map/reduce_sum | solution.py:339
  93.9 0.1 rsqrt.11
  94.0 0.0 copy-done.5
  94.0 0.1 fusion.20
  94.1 0.1 fusion.77
  94.2 0.2 select_reduce_fusion
  94.4 0.0 copy-done.4
  94.4 0.1 reduce.1
  94.5 3.2 %fusion.7 = bf16[2,160,4096]{2,1,0:T(8,128)(2,1)S(1)} fusion(bf16[2,256,4096]{2,1,0:T(8,128)(2,1)} %bitcast.120, f32[2,4096]{1,0:T(2,128)S(1)} %mul.159, f32[160]{0:T(256)S(1)} %get-tuple-element.20, s32[256]{0:T(256)S(1)} %fusion.20), kind=kOutput, calls=%fused_computation.8 | convolution fusion | flops 675061760 | bytes 6850176 | tf_op jit(solution)/shard_map/rt,ctd->crd/dot_general | solution.py:353
  97.7 0.0 copy-start.7
  97.7 12.3 %convolution_bitcast_fusion.1 = f32[160,1536]{1,0:T(8,128)} fusion(bf16[2,160,4096]{2,1,0:T(8,128)(2,1)S(1)} %fusion.7, bf16[2,4096,1536]{2,1,0:T(8,128)(2,1)} %bitcast.132), kind=kOutput, calls=%fused_computation.15 | convolution fusion | flops 4026531840 | bytes 28770304 | tf_op jit(solution)/shard_map/crd,cdh->rh/dot_general | solution.py:357
  110.0 0.0 copy-done.7
  110.0 20.0 %fusion.2 = bf16[160,8192]{1,0:T(8,128)(2,1)S(1)} fusion(bf16[1,1536,8192]{2,1,0:T(8,128)(2,1)} %param.25, bf16[2,160,4096]{2,1,0:T(8,128)(2,1)} %copy-done.7, bf16[2,4096,1536]{2,1,0:T(8,128)(2,1)} %bitcast.133, f32[160,1536]{1,0:T(8,128)} %convolution_bitcast_fusion.1, f32[160]{0:T(256)S(1)} %get-tuple-element.19), kind=kOutput, calls=%fused_computation.2 | convolution fusion | flops 8056094720 | bytes 56558208 | tf_op jit(solution)/shard_map/dot_general | solution.py:360
  130.0 3.4 %convolution_convert_fusion.1 = bf16[16,512,256]{1,2,0:T(8,128)(2,1)} fusion(bf16[20,16,8,512]{3,2,1,0:T(8,128)(2,1)S(1)} %bitcast.122, s32[256]{0:T(256)S(1)} %fusion.20), kind=kOutput, calls=%fused_computation.9 | convolution fusion | flops 673226752 | bytes 6816768 | tf_op jit(solution)/shard_map/rt,rgd->gtd/dot_general | solution.py:361
  133.4 32.0 %scatter3.1 = f32[128,512]{1,0:T(8,128)} custom-call(bf16[4,2,2,2,128,512]{5,4,3,2,1,0:T(8,128)(2,1)} %bitcast.118), custom_call_target="tpu_custom_call" | custom-call | tf_op jit(solution)/shard_map/scatter3/pallas_call | solution.py:208
  165.5 1.7 fusion.32
  (8 shorter events, 0.2 us)
Async XLA Ops:
  0.0 23.9 %copy-start.6 = (f32[4]{0:T(128)S(1)}, f32[4]{0:T(128)}, u32[]{:S(2)}) copy-start(f32[4]{0:T(128)} %param.18) | copy-start | bytes 52
  18.0 5.4 %copy-start.2 = (bf16[2,128,128]{2,1,0:T(8,128)(2,1)S(1)}, bf16[2,128,128]{2,1,0:T(8,128)(2,1)}, u32[]{:S(2)}) copy-start(bf16[2,128,128]{2,1,0:T(8,128)(2,1)} %get-tuple-element.14) | copy-start | bytes 196612
  18.0 5.4 %copy-start.3 = (bf16[2,128,128]{2,1,0:T(8,128)(2,1)S(1)}, bf16[2,128,128]{2,1,0:T(8,128)(2,1)}, u32[]{:S(2)}) copy-start(bf16[2,128,128]{2,1,0:T(8,128)(2,1)} %get-tuple-element.13) | copy-start | bytes 196612
  25.1 5.8 %copy-start.1 = (bf16[2,128,512]{2,1,0:T(8,128)(2,1)S(1)}, bf16[2,128,512]{2,1,0:T(8,128)(2,1)}, u32[]{:S(2)}) copy-start(bf16[2,128,512]{2,1,0:T(8,128)(2,1)} %get-tuple-element.16) | copy-start | bytes 786436
  31.0 63.0 %copy-start.5 = (f32[2,8,128]{2,1,0:T(8,128)S(1)}, f32[2,8,128]{2,1,0:T(8,128)}, u32[]{:S(2)}) copy-start(f32[2,8,128]{2,1,0:T(8,128)} %get-tuple-element.15) | copy-start | bytes 24580
  33.7 1.4 copy-start
  90.8 3.6 %copy-start.4 = (f32[4,2,2,1,512]{4,3,2,1,0:T(1,128)S(1)}, f32[4,2,2,1,512]{4,3,2,1,0:T(1,128)}, u32[]{:S(2)}) copy-start(f32[4,2,2,1,512]{4,3,2,1,0:T(1,128)} %get-tuple-element.18) | copy-start | bytes 98308
  97.7 12.3 %copy-start.7 = (bf16[2,160,4096]{2,1,0:T(8,128)(2,1)}, bf16[2,160,4096]{2,1,0:T(8,128)(2,1)S(1)}, u32[]{:S(2)}) copy-start(bf16[2,160,4096]{2,1,0:T(8,128)(2,1)S(1)} %fusion.7) | copy-start | bytes 7864324

commit v3 on v2

--- a/solution.py
+++ b/solution.py
@@ -331,12 +331,14 @@
     jobs = [(0, whole, order, cut[k]) for k in range(2) for order, cut in zip(orders, cuts)]
     spread_over = state + expert_down
     jobs.append((1, spread_over, spread_over, (0, block)))
-    resid, gain = gather([resid_piece, norm_gain[None, :]], jobs, 2)
+    squares = jnp.sum(resid_piece.astype(jnp.float32) ** 2, axis=1)[None, :]
+    jobs.append((2, whole, state + ctx + side + core, (0, rows)))
+    resid, gain, squares = gather([resid_piece, norm_gain[None, :], squares], jobs, 2)
+    squares = squares.reshape(n_ctx, count)
     gain = gain.reshape(n_ctx, 1, half)
     resid = resid.reshape(n_ctx, count, half)
 
-    wide = resid.astype(jnp.float32)
-    scale = lax.rsqrt(jnp.sum(wide * wide, axis=(0, 2)) / width + norm_epsilon)
+    scale = lax.rsqrt(jnp.sum(squares, axis=0) / width + norm_epsilon)
 
     routed = all_routes == expert_at
     chosen = jnp.any(routed, axis=2)

time: 168 us -> 168 us (level)
  no operation moved by 1% of the time
where the time goes in v3:
time: 168 us; the launch traced here: 167 us
  Pallas kernels  104 us (62%)
  matrix products  48.6 us (29%)
  other arithmetic  7.77 us (5%)
  local copies, waits for them, and re-layouts  6.64 us (4%)
    pallas_call x2, Pallas kernels, scatter(): pl.pallas_call(functools.partial(scatter_kernel, dims, parts), out_shape=...  55.5 us
    pallas_call x2, Pallas kernels, gather(): pl.pallas_call(functools.partial(gather_kernel, jobs, used, len(arrays)),...  48.5 us
    dot_general x1, matrix products, shards(): jnp.dot(hidden, w_down[0], preferred_element_type=jnp.float32)  20 us
    dot_general x1, matrix products, shards(): jnp.einsum('crd,cdh->rh', entering, gate_parts, preferred_element_type=jn...  12.3 us
    dot_general x1, matrix products, shards(): jnp.dot(all_mixed, out_proj, preferred_element_type=jnp.float32)  5.8 us

profile of v3, /device:TPU:0, one launch (start us, length us, event | category | flops | bytes accessed | tf_op | source)
XLA Modules:
  0.0 167.3 jit_solution(16878924255445354051)
XLA Ops:
  0.0 0.0 copy-start.5
  0.0 0.7 convert_bitcast_fusion
  0.7 1.3 pad_maximum_fusion.refs_3_
  2.0 16.0 %gather0.1 = (bf16[2,128,1024]{2,1,0:T(8,128)(2,1)}, bf16[2,128,128]{2,1,0:T(8,128)(2,1)}, bf16[2,128,128]{2,1,0:T(8,128)(2,1)}, f32[2,8,128]{2,1,0:T(8,128)}, bf16[2,128,512]{2,1,0:T(8,128)(2,1)}) custom-call(bf16[128,1024]{1,0:T(8,128)(2,1)} %refs_0_.1, bf16[128,128]{1,0:T(8,128)(2,1)} %refs_1_.1, bf16[128,128]{1,0:T(8,128)(2,1)} %refs_2_.1, ...), custom_call_target="tpu_custom_call" | custom-call | tf_op jit(solution)/shard_map/gather0/pallas_call | solution.py:106
  18.0 0.0 copy-start.2
  18.0 0.0 copy-start.3
  18.0 0.7 slice_bitcast_fusion
  18.8 0.1 copy.14
  18.9 0.2 reduce_window_sum.17
  19.1 0.1 copy.15
  19.1 0.1 sqrt_multiply_fusion
  19.2 1.1 fusion.82
  20.3 0.2 copy.29
  20.5 1.2 convolution_bitcast_fusion.2
  21.7 0.1 copy.19
  21.8 0.2 reduce_window_sum.18
  22.0 0.1 copy.24
  22.1 1.4 convolution_multiply_fusion.1
  23.4 0.0 copy-done.2
  23.4 0.0 copy-done.3
  23.5 0.1 fusion.65
  23.6 0.1 copy.20
  23.7 0.2 copy.30
  23.9 0.0 copy-done.5
  23.9 0.5 fusion.16
  24.4 0.1 fusion.68
  24.6 0.5 fusion.17
  25.1 0.0 copy-start.1
  25.1 5.8 %convolution_convert_fusion = bf16[256,4096]{1,0:T(8,128)(2,1)S(1)} fusion(bf16[1024,4096]{1,0:T(8,128)(2,1)} %param.19, bf16[128,1024]{0,1:T(8,128)(2,1)S(1)} %bitcast.125, bf16[128,1024]{0,1:T(8,128)(2,1)S(1)} %bitcast.126), kind=kOutput, calls=%fused_computation.6 | convolution fusion | flops 2149580800 | bytes 11010048 | tf_op jit(solution)/shard_map/dot_general | solution.py:308
  30.9 0.0 copy-start.4
  31.0 0.0 copy-done.1
  31.0 0.1 convert_select_fusion
  31.0 0.1 fusion.29
  31.2 2.5 %dynamic_update_slice.3 = bf16[256,4096]{1,0:T(8,128)(2,1)S(1)} dynamic-update-slice(bf16[256,4096]{1,0:T(8,128)(2,1)S(1)} %convolution_convert_fusion, bf16[256,512]{1,0:T(8,128)(2,1)S(1)} %fusion.29, s32[]{:T(128)} %constant.54.clone.1, s32[]{:T(128)S(6)} %min.12) | dynamic-update-slice | bytes 524292 | tf_op jit(solution)/shard_map/dynamic_update_slice | solution.py:314
  33.7 0.0 copy-start
  33.7 1.3 copy-done
  35.0 23.4 %scatter1.1.refs_0_ = bf16[16,4096]{1,0:T(8,128)(2,1)} custom-call(bf16[4,2,2,16,4096]{4,3,2,1,0:T(8,128)(2,1)} %bitcast.120), custom_call_target="tpu_custom_call" | custom-call | tf_op jit(solution)/shard_map/scatter1/pallas_call | solution.py:208
  58.5 1.6 multiply_reduce_fusion
  60.0 32.5 %gather2.1 = (bf16[2,4,2,2,16,4096]{5,4,3,2,1,0:T(8,128)(2,1)}, f32[4,2,2,1,512]{4,3,2,1,0:T(1,128)}, f32[2,4,2,2,1,16]{5,4,3,2,1,0:T(1,128)}) custom-call(bf16[16,4096]{1,0:T(8,128)(2,1)} %scatter1.1.refs_0_, f32[1,512]{1,0:T(1,128)} %bitcast.130, f32[1,16]{1,0:T(1,128)} %bitcast.131), custom_call_target="tpu_custom_call" | custom-call | tf_op jit(solution)/shard_map/gather2/pallas_call | solution.py:106
  92.5 0.8 reduce_sum.46
  93.3 0.1 rsqrt.11
  93.4 0.0 copy-done.4
  93.4 0.1 fusion.20
  93.5 0.1 fusion.77
  93.6 0.2 select_reduce_fusion
  93.8 0.9 reduce.2
  94.7 3.2 %fusion.7 = bf16[2,160,4096]{2,1,0:T(8,128)(2,1)S(1)} fusion(bf16[2,256,4096]{2,1,0:T(8,128)(2,1)} %bitcast.127, f32[2,4096]{1,0:T(2,128)S(1)} %mul.154, f32[160]{0:T(256)S(1)} %get-tuple-element.22, s32[256]{0:T(256)S(1)} %fusion.20), kind=kOutput, calls=%fused_computation.7 | convolution fusion | flops 675061760 | bytes 6850176 | tf_op jit(solution)/shard_map/rt,ctd->crd/dot_general | solution.py:355
  97.9 0.0 copy-start.6
  97.9 12.3 %convolution_bitcast_fusion.1 = f32[160,1536]{1,0:T(8,128)} fusion(bf16[2,160,4096]{2,1,0:T(8,128)(2,1)S(1)} %fusion.7, bf16[2,4096,1536]{2,1,0:T(8,128)(2,1)} %bitcast.134), kind=kOutput, calls=%fused_computation.14 | convolution fusion | flops 4026531840 | bytes 28770304 | tf_op jit(solution)/shard_map/crd,cdh->rh/dot_general | solution.py:359
  110.2 0.0 copy-done.6
  110.2 20.0 %fusion.2 = bf16[160,8192]{1,0:T(8,128)(2,1)S(1)} fusion(bf16[1,1536,8192]{2,1,0:T(8,128)(2,1)} %param.25, bf16[2,160,4096]{2,1,0:T(8,128)(2,1)} %copy-done.6, bf16[2,4096,1536]{2,1,0:T(8,128)(2,1)} %bitcast.135, f32[160,1536]{1,0:T(8,128)} %convolution_bitcast_fusion.1, f32[160]{0:T(256)S(1)} %get-tuple-element.21), kind=kOutput, calls=%fused_computation.2 | convolution fusion | flops 8056094720 | bytes 56558208 | tf_op jit(solution)/shard_map/dot_general | solution.py:362
  130.2 3.4 %convolution_convert_fusion.1 = bf16[16,512,256]{1,2,0:T(8,128)(2,1)} fusion(bf16[20,16,8,512]{3,2,1,0:T(8,128)(2,1)S(1)} %bitcast.121, s32[256]{0:T(256)S(1)} %fusion.20), kind=kOutput, calls=%fused_computation.8 | convolution fusion | flops 673226752 | bytes 6816768 | tf_op jit(solution)/shard_map/rt,rgd->gtd/dot_general | solution.py:363
  133.5 32.0 %scatter3.1 = f32[128,512]{1,0:T(8,128)} custom-call(bf16[4,2,2,2,128,512]{5,4,3,2,1,0:T(8,128)(2,1)} %bitcast.119), custom_call_target="tpu_custom_call" | custom-call | tf_op jit(solution)/shard_map/scatter3/pallas_call | solution.py:208
  165.6 1.7 fusion.32
  (8 shorter events, 0.1 us)
Async XLA Ops:
  0.0 23.9 %copy-start.5 = (f32[4]{0:T(128)S(1)}, f32[4]{0:T(128)}, u32[]{:S(2)}) copy-start(f32[4]{0:T(128)} %param.18) | copy-start | bytes 52
  18.0 5.4 %copy-start.2 = (bf16[2,128,128]{2,1,0:T(8,128)(2,1)S(1)}, bf16[2,128,128]{2,1,0:T(8,128)(2,1)}, u32[]{:S(2)}) copy-start(bf16[2,128,128]{2,1,0:T(8,128)(2,1)} %get-tuple-element.15) | copy-start | bytes 196612
  18.0 5.4 %copy-start.3 = (bf16[2,128,128]{2,1,0:T(8,128)(2,1)S(1)}, bf16[2,128,128]{2,1,0:T(8,128)(2,1)}, u32[]{:S(2)}) copy-start(bf16[2,128,128]{2,1,0:T(8,128)(2,1)} %get-tuple-element.14) | copy-start | bytes 196612
  25.1 5.8 %copy-start.1 = (bf16[2,128,512]{2,1,0:T(8,128)(2,1)S(1)}, bf16[2,128,512]{2,1,0:T(8,128)(2,1)}, u32[]{:S(2)}) copy-start(bf16[2,128,512]{2,1,0:T(8,128)(2,1)} %get-tuple-element.17) | copy-start | bytes 786436
  30.9 62.5 %copy-start.4 = (f32[2,8,128]{2,1,0:T(8,128)S(1)}, f32[2,8,128]{2,1,0:T(8,128)}, u32[]{:S(2)}) copy-start(f32[2,8,128]{2,1,0:T(8,128)} %get-tuple-element.16) | copy-start | bytes 24580
  33.7 1.4 copy-start
  97.9 12.3 %copy-start.6 = (bf16[2,160,4096]{2,1,0:T(8,128)(2,1)}, bf16[2,160,4096]{2,1,0:T(8,128)(2,1)S(1)}, u32[]{:S(2)}) copy-start(bf16[2,160,4096]{2,1,0:T(8,128)(2,1)S(1)} %fusion.7) | copy-start | bytes 7864324
